TPU v7x, 768 devices: a whole 4x8x12 slice. The times are simulated.
768 devices in a mesh: dp: 96 (over z_lo, y, core), expert: 8 (over x, z_hi).
Axes of the slice: x: 4, y: 8, z: 12 (z_hi: 2, z_lo: 6; z = z_hi * 6 + z_lo), core: 2. Of those that a mesh axis runs over, the one named last changes fastest.
Arguments:
- grad_out: bfloat16 [196608, 3072], P(('dp', 'expert')), may hold values from -1.5 to 1.5
- routes: int32 [196608, 2], P(('dp', 'expert')), may hold values from 0 to 63, as said below
- gate_levels: int32 [196608, 2], P(('dp', 'expert')), may hold values from 1 to 15
- saved_inputs: bfloat16 [73728, 3072], P(('dp', 'expert')), may hold values from -6 to 6
- w_gate: bfloat16 [3072, 2048], P(None, 'expert'), may hold values from -0.109375 to 0.109375
- w_up: bfloat16 [3072, 2048], P(None, 'expert'), may hold values from -0.109375 to 0.109375
- w_down: bfloat16 [2048, 3072], P('expert'), may hold values from -0.1875 to 0.1875
Outputs:
- input_grad: bfloat16 [196608, 3072], P(('dp', 'expert'))
- gate_grad: float32 [196608, 2], P(('dp', 'expert'))
- weight_grad: float32 [3072, 3, 2048], P('dp', None, 'expert')
Inputs may be any that keep to these rules, and one draw needn't show every extreme that they name: `routes`: the ids of one token differ. A device's tokens name each expert below 2 at most 12 times; in every block one of them is named exactly 12 times, and the same one for all 8 blocks of one replica.
All inputs are finite; a program needn't handle non-finite values.
Results may differ from a plain program's by a relative error of at most 0.012.
Values may be sent and summed in bfloat16 or wider, within the bound.
A program may use at most 128 MiB of HBM per device.

v0:
```python
import jax
import jax.numpy as jnp
from jax import lax
from jax.sharding import PartitionSpec as P

EXPERTS_W = 2


def rows_product(left, right):
    return lax.dot_general(
        left, right, (((0,), (0,)), ((), ())), preferred_element_type=jnp.float32
    )


def back_product(left, right):
    return lax.dot_general(
        left, right, (((1,), (1,)), ((), ())), preferred_element_type=jnp.float32
    )


def per_device(grad_out, routes, gate_levels, saved_inputs, w_gate, w_up, w_down):
    group = lax.axis_size("expert")
    shards = group // EXPERTS_W
    capacity = saved_inputs.shape[0] // group
    width = grad_out.shape[1]
    hits = (routes[:, :, None] == jnp.arange(EXPERTS_W, dtype=jnp.int32)).astype(jnp.int32)
    member = jnp.sum(hits, axis=1)
    levels = jnp.sum(hits * gate_levels[:, :, None], axis=1)
    slots = jnp.cumsum(member, axis=0) - 1
    placed = (member[None] == 1) & (
        slots[None] == jnp.arange(capacity, dtype=jnp.int32)[:, None, None]
    )
    table = jnp.transpose(placed, (2, 0, 1))
    table_half = table.astype(jnp.bfloat16)
    table_full = table.astype(jnp.float32)
    picked = jnp.einsum(
        "ect,td->ecd", table_half, grad_out, preferred_element_type=jnp.float32
    ).astype(jnp.bfloat16)
    slot_gate = (
        jnp.einsum(
            "ect,te->ec", table_full, levels.astype(jnp.float32), precision=lax.Precision.HIGHEST
        )
        / 16.0
    )
    send_rows = jnp.repeat(picked, shards, axis=0)
    send_gate = jnp.repeat(slot_gate, shards, axis=0).astype(jnp.bfloat16)
    recv_rows, recv_gate = (
        lax.all_to_all(send_rows, "expert", split_axis=0, concat_axis=0, tiled=True),
        lax.all_to_all(send_gate, "expert", split_axis=0, concat_axis=0, tiled=True),
    )
    grad_rows = recv_rows.reshape(group * capacity, width)
    gates = recv_gate.reshape(group * capacity, 1).astype(jnp.float32)
    pre_gate = jnp.dot(saved_inputs, w_gate, preferred_element_type=jnp.float32)
    pre_up = jnp.dot(saved_inputs, w_up, preferred_element_type=jnp.float32)
    projected = back_product(grad_rows, w_down)
    sigma = jax.nn.sigmoid(pre_gate)
    activ = pre_gate * sigma
    hidden = activ * pre_up
    gate_part = jnp.sum(hidden * projected, axis=1).astype(jnp.bfloat16)
    d_hidden = gates * projected
    d_up = (d_hidden * activ).astype(jnp.bfloat16)
    d_pre = (d_hidden * pre_up * sigma * (1.0 + pre_gate * (1.0 - sigma))).astype(jnp.bfloat16)
    scaled_hidden = (gates * hidden).astype(jnp.bfloat16)
    input_part = (back_product(d_pre, w_gate) + back_product(d_up, w_up)).astype(jnp.bfloat16)
    back_rows, back_gate = (
        lax.all_to_all(
            input_part.reshape(group, capacity, width),
            "expert",
            split_axis=0,
            concat_axis=0,
            tiled=True,
        ),
        lax.all_to_all(
            gate_part.reshape(group, capacity), "expert", split_axis=0, concat_axis=0, tiled=True
        ),
    )
    gate_share = lax.psum_scatter(
        rows_product(saved_inputs, d_pre), "dp", scatter_dimension=0, tiled=True
    )
    up_share = lax.psum_scatter(
        rows_product(saved_inputs, d_up), "dp", scatter_dimension=0, tiled=True
    )
    down_share = lax.psum_scatter(
        rows_product(grad_rows, scaled_hidden), "dp", scatter_dimension=0, tiled=True
    )
    weight_grad = jnp.stack([gate_share, up_share, down_share], axis=1)
    summed = back_rows.astype(jnp.float32).reshape(EXPERTS_W, shards, capacity, width).sum(axis=1)
    gate_summed = back_gate.astype(jnp.float32).reshape(EXPERTS_W, shards, capacity).sum(axis=1)
    input_grad = jnp.einsum(
        "ect,ecd->td", table_full, summed, precision=lax.Precision.HIGHEST
    ).astype(jnp.bfloat16)
    per_expert = jnp.einsum("ect,ec->te", table_full, gate_summed, precision=lax.Precision.HIGHEST)
    gate_grad = jnp.sum(hits.astype(jnp.float32) * per_expert[:, None, :], axis=2)
    return (input_grad, gate_grad, weight_grad)


def solution(mesh):
    in_specs = (
        P(("dp", "expert"), None),
        P(("dp", "expert"), None),
        P(("dp", "expert"), None),
        P(("dp", "expert"), None),
        P(None, "expert"),
        P(None, "expert"),
        P("expert", None),
    )
    out_specs = (P(("dp", "expert"), None), P(("dp", "expert"), None), P("dp", None, "expert"))
    return jax.shard_map(
        per_device, mesh=mesh, in_specs=in_specs, out_specs=out_specs, check_vma=False
    )
```

profile of v0, /device:TPU:1, one launch (start us, length us, event | category | flops | bytes accessed | tf_op | source)
XLA Modules:
  0.0 1779.1 jit_solution(6431923530075115528)
XLA Ops:
  9.9 17.5 all-to-all-start
  27.4 1.8 convolution_convert_fusion
  29.2 9.4 all-to-all-done
  38.7 1.0 broadcast_in_dim.5
  39.6 3.5 all-to-all-start.1
  43.2 2.4 fusion.26
  45.7 1.0 fusion.27
  46.8 13.8 all-to-all-done.1
  60.8 2.2 multiply_reduce_fusion
  63.0 2.3 convolution_bitcast_fusion.1
  65.3 3.5 copy.39
  68.9 2.3 convolution_bitcast_fusion
  71.2 3.6 copy.41
  75.7 2.3 fusion.4
  78.8 3.3 all-to-all-start.3
  82.7 1.4 fusion.1
  84.1 2.1 reshape.89
  86.2 7.0 all-to-all-done.3
  93.2 4.3 all-to-all-start.2
  98.4 14.7 all-to-all-done.2
  113.2 2.6 fusion
  115.8 534.1 %reduce-scatter.10.cloned.1.call-done = f32[32,256]{1,0:T(8,128)} async-done(((f32[3072,256]{1,0:T(8,128)}), f32[32,256]{1,0:T(8,128)}) %reduce-scatter.10.cloned.1.call-update) | async-done | bytes 32784
  650.8 560.3 %reduce-scatter.12.cloned.1.call-done = f32[32,256]{1,0:T(8,128)} async-done(((f32[3072,256]{1,0:T(8,128)}), f32[32,256]{1,0:T(8,128)}) %reduce-scatter.12.cloned.1.call-update) | async-done | bytes 32784
  1212.0 559.0 %reduce-scatter.14.cloned.1.call-done = f32[32,256]{1,0:T(8,128)} async-done(((f32[3072,256]{1,0:T(8,128)}), f32[32,256]{1,0:T(8,128)}) %reduce-scatter.14.cloned.1.call-update) | async-done | bytes 32784
  (49 shorter events, 9.6 us)
Async XLA Ops:
  7.2 38.5 %copy-start = (bf16[3072,256]{1,0:T(8,128)(2,1)S(1)}, bf16[3072,256]{1,0:T(8,128)(2,1)}, u32[]{:S(2)}) copy-start(bf16[3072,256]{1,0:T(8,128)(2,1)} %param.11) | copy-start | bytes 4718596
  9.9 28.8 %all-to-all-start = ((bf16[8,1,12]{2,1,0:T(2,128)(2,1)}), bf16[8,1,12]{2,1,0:T(2,128)(2,1)S(1)}, u32[]{:S(2)}, u32[]{:S(2)}) async-start(bf16[8,1,12]{2,1,0:T(2,128)(2,1)} %copy.27), calls=%async_computation | async-start | bytes 8192 | tf_op jit(solution)/shard_map/all_to_all | solution.py:49
  29.2 14.0 copy-start.1
  39.6 21.0 %all-to-all-start.1 = ((bf16[8,12,3072]{2,1,0:T(8,128)(2,1)}), bf16[8,12,3072]{2,1,0:T(8,128)(2,1)S(1)}, u32[]{:S(2)}, u32[]{:S(2)}) async-start(bf16[8,12,3072]{2,1,0:T(8,128)(2,1)} %bitcast.61), calls=%async_computation.1 | async-start | bytes 1572864 | tf_op jit(solution)/shard_map/all_to_all | solution.py:48
  43.2 606.7 %reduce-scatter.10.cloned.1.call-start = ((), (), s32[]{:S(2)}) async-start(), calls=%async_computation.7 | async-start | bytes 3178496
  68.8 1142.2 %reduce-scatter.12.cloned.1.call-start = ((), (), s32[]{:S(2)}) async-start(), calls=%async_computation.8 | async-start | bytes 3178496
  74.8 0.9 copy-start.3
  74.8 0.9 copy-start.4
  74.8 1696.2 %reduce-scatter.14.cloned.1.call-start = ((), (), s32[]{:S(2)}) async-start(), calls=%async_computation.9 | async-start | bytes 3178496
  78.1 4.6 copy-start.2
  78.8 14.5 all-to-all-start.3
  84.1 13.6 copy-start.5
  93.2 19.8 %all-to-all-start.2 = ((bf16[8,12,3072]{2,1,0:T(8,128)(2,1)}), bf16[8,12,3072]{2,1,0:T(8,128)(2,1)S(1)}, u32[]{:S(2)}, u32[]{:S(2)}) async-start(bf16[8,12,3072]{2,1,0:T(8,128)(2,1)} %reshape.89), calls=%async_computation.2 | async-start | bytes 1572864 | tf_op jit(solution)/shard_map/all_to_all | solution.py:66
Sparse Core Ops, SparseCore 0:
  69.0 580.8 reduce-scatter.9
  653.3 557.7 reduce-scatter.11
  1214.2 556.7 reduce-scatter.13
where the time goes:
time: 1790 us; the launch traced here: 1780 us
  waiting for transfers between devices  1700 us (95%)
  starting transfers between devices  28.8 us (2%)
  matrix products  19.2 us (1%)
    unnamed x6, waiting for transfers between devices  1650 us
  transfers between devices with their start and end apart: 7, of which 7 were waited for; matrix products, arithmetic and copies ran while one was open for 1% of the time, Pallas kernels for 0%

commit v1 on v0

v1 whole, which is shorter than its diff:
```python
import functools

import jax
import jax.numpy as jnp
from jax import lax
from jax.experimental import pallas as pl
from jax.experimental.pallas import tpu as pltpu
from jax.sharding import PartitionSpec as P

NY, NC, NH = 8, 2, 2
SLAB = 16
LANES = 128
BF, F32 = jnp.bfloat16, jnp.float32


def nt(a, b):
    return lax.dot_general(a, b, (((1,), (1,)), ((), ())), preferred_element_type=F32)


def nn(a, b):
    return lax.dot_general(a, b, (((1,), (0,)), ((), ())), preferred_element_type=F32)


def kernel(
    nx, nz, cap,
    routes_ref, levels_ref, go_hbm, x_hbm, wg_hbm, wu_hbm, wd_hbm,
    ig_hbm, gg_ref, wgr_ref,
    go, xv, wg, wu, wd, ig,
    pl_ref, plt_ref, pk, zin, dyin, xp, xt, xty, act, hid, dfac,
    nar, gp_in, gm_in, g4_in, dab, hg, ip, ret, zsum, zrin, dyt,
    gds, gdr, gdo, psend, prr, msend, mrr, p0r, m0r, sd, gx, gxr, sx,
    zsd, zrd, zsx, zrx, loc_sem, send_sem, recv_sem,
):
    dp, ex = lax.axis_index("dp"), lax.axis_index("expert")
    core = lax.rem(dp, NC)
    y = lax.rem(lax.div(dp, NC), NY)
    z = lax.div(dp, NC * NY)
    h = lax.rem(ex, NH)
    x = lax.div(ex, NH)
    width = go.shape[1]
    rows = dyin.shape[0] * SLAB
    zw = width // nz
    yw = zw // NY
    cw = yw // NC
    half = nz * cw // 2

    def x_dev(d):
        return (dp, lax.rem(x + d, nx) * NH + h)

    h_dev = (dp, x * NH + (1 - h))

    def y_dev(d):
        return ((z * NY + lax.rem(y + d, NY)) * NC + core, ex)

    c_dev = ((z * NY + y) * NC + (1 - core), ex)

    def z_dev(d):
        return ((lax.rem(z + d, nz) * NY + y) * NC + core, ex)

    started = []

    def send(src, dst, dev):
        i = len(started)
        copy = pltpu.make_async_remote_copy(
            src_ref=src, dst_ref=dst, send_sem=send_sem.at[i], recv_sem=recv_sem.at[i],
            device_id=dev, device_id_type=pl.DeviceIdType.MESH,
        )
        copy.start()
        started.append(copy)
        return copy

    loads = [
        pltpu.make_async_copy(src, dst, loc_sem.at[i])
        for i, (src, dst) in enumerate(
            [(go_hbm, go), (x_hbm, xv), (wg_hbm, wg), (wu_hbm, wu), (wd_hbm, wd)]
        )
    ]
    for load in loads:
        load.start()
    barrier = pltpu.get_barrier_semaphore()
    partners = (
        [h_dev] + [x_dev(d) for d in range(1, nx)] + [y_dev(d) for d in range(1, NY)]
        + [c_dev] + [z_dev(d) for d in range(1, nz)]
    )
    for dev in partners:
        pl.semaphore_signal(barrier, inc=1, device_id=dev, device_id_type=pl.DeviceIdType.MESH)

    toks = go.shape[0]
    r = routes_ref[...]
    lv = levels_ref[...].astype(F32)
    r0, r1, l0, l1 = r[0:1], r[1:2], lv[0:1], lv[1:2]
    mem = [jnp.where((r0 == e) | (r1 == e), 1.0, 0.0) for e in range(2)]
    lev = [jnp.where(r0 == e, l0, 0.0) + jnp.where(r1 == e, l1, 0.0) for e in range(2)]
    row8 = lax.broadcasted_iota(jnp.int32, (8, toks), 0)
    m8 = jnp.where(row8 == 0, mem[0], jnp.where(row8 == 1, mem[1], 0.0)).astype(BF)
    tri = jnp.where(
        lax.broadcasted_iota(jnp.int32, (toks, toks), 0)
        <= lax.broadcasted_iota(jnp.int32, (toks, toks), 1), 1.0, 0.0,
    ).astype(BF)
    slots = nn(m8, tri) - 1.0
    row = lax.broadcasted_iota(jnp.int32, (2 * SLAB, toks), 0)
    first = row < SLAB
    want = jnp.where(first, row, row - SLAB).astype(F32)
    slot_row = jnp.where(first, slots[0:1], slots[1:2])
    mem_row = jnp.where(first, mem[0], mem[1])
    lev_row = jnp.where(first, lev[0], lev[1])
    placed = jnp.where((mem_row > 0.5) & (slot_row == want), 1.0, 0.0)
    pl_ref[...] = placed
    gate = jnp.sum(placed * lev_row, axis=1, keepdims=True) * (1.0 / 16.0)
    pk[:, width:] = jnp.broadcast_to(gate, (2 * SLAB, LANES)).astype(BF)
    placed_b = placed.astype(BF)
    loads[0].wait()
    for c in range(0, width, 512):
        pk[:, c:c + 512] = nn(placed_b, go[:, c:c + 512]).astype(BF)

    cols = [(0, width // 2), (width // 2, width // 2 + LANES)]
    mine, other = x * NH + h, x * NH + (1 - h)
    pl.semaphore_wait(barrier, len(partners))
    z_in = [send(pk.at[:, pl.ds(a, w)], zin.at[:, pl.ds(a, w)], h_dev) for a, w in cols]

    def spread(src, slab, a, w):
        got = []
        for d in range(1, nx):
            e = lax.div(lax.rem(x + d, nx), nx // 2)
            lo = pl.multiple_of(e * SLAB, SLAB)
            got.append(send(src.at[pl.ds(lo, SLAB), pl.ds(a, w)],
                            dyin.at[slab, :, pl.ds(a, w)], x_dev(d)))
        return got

    own = pl.multiple_of(lax.div(x, nx // 2) * SLAB, SLAB)
    dy_own = [spread(pk, mine, a, w) for a, w in cols]
    dyin[mine] = pk[pl.ds(own, SLAB), :]

    loads[1].wait()
    n_rows = xv.shape[0]
    pad = jnp.zeros((LANES - n_rows, zw), BF)
    for b in range(nz):
        xt[b] = jnp.concatenate([xv[:, b * zw:(b + 1) * zw], pad], axis=0).T
    x_in = []
    for d in range(1, NY):
        lo = pl.multiple_of(lax.rem(y + d, NY) * yw, yw)
        x_in.append(send(xt.at[:, pl.ds(lo, yw), :], xty.at[d - 1], y_dev(d)))
    gi = lax.broadcasted_iota(jnp.int32, (rows, n_rows), 0)
    gk = lax.broadcasted_iota(jnp.int32, (rows, n_rows), 1)
    gc = jnp.bitwise_and(gi, SLAB - 1)
    gs = jnp.right_shift(gi, 4)
    widen = jnp.where((gc < cap) & (gk == gs * cap + gc), 1.0, 0.0).astype(BF)
    ni = lax.broadcasted_iota(jnp.int32, (n_rows, rows), 0)
    nk = lax.broadcasted_iota(jnp.int32, (n_rows, rows), 1)
    nc_ = jnp.bitwise_and(nk, SLAB - 1)
    ns = jnp.right_shift(nk, 4)
    narrow = jnp.where((nc_ < cap) & (ni == ns * cap + nc_), 1.0, 0.0).astype(BF)
    for c in range(0, width, 512):
        xp[:, c:c + 512] = nn(widen, xv[:, c:c + 512]).astype(BF)
    loads[2].wait()
    a_pre = nn(xp[...], wg[...])
    loads[3].wait()
    b_pre = nn(xp[...], wu[...])
    sigma = jax.nn.sigmoid(a_pre)
    activ = a_pre * sigma
    act[...] = activ
    hid[...] = activ * b_pre
    dfac[...] = b_pre * sigma * (1.0 + a_pre * (1.0 - sigma))
    pl_two = jnp.concatenate(
        [pl_ref[...], pl_ref[...], jnp.zeros((LANES - 4 * SLAB, toks), F32)], axis=0)
    plt_ref[...] = pl_two.T.astype(BF)

    dy_other = []
    for k, (a, w) in enumerate(cols):
        z_in[k].wait_recv()
        dy_other.append(spread(zin, other, a, w))
    dyin[other] = zin[pl.ds(own, SLAB), :]
    loads[4].wait()
    proj = jnp.zeros((rows, wd.shape[0]), F32)
    for k, (a, w) in enumerate(cols):
        for copy in dy_own[k] + dy_other[k]:
            copy.wait_recv()
        for c in range(a, a + width // 2, 512):
            proj += nt(dyin[:, :, c:c + 512].reshape(rows, 512), wd[:, c:c + 512])
    g_half = dyin[:, :, width:].reshape(rows, LANES).astype(F32)
    g = jnp.concatenate([g_half, g_half], axis=1)
    d_hid = g * proj
    dab[:, 256:] = (d_hid * act[...]).astype(BF)
    dab[:, :256] = (d_hid * dfac[...]).astype(BF)
    hg[...] = (g * hid[...]).astype(BF)
    gate_part = jnp.sum(hid[...] * proj, axis=1, keepdims=True).astype(BF)

    nar[...] = nn(narrow, dab[...]).astype(BF)
    hr = n_rows // 2
    up = [send(nar, gp_in.at[0], y_dev(1))]
    down = [send(nar, gm_in.at[0], y_dev(NY - 1))]

    for c in range(0, width, 512):
        part = nt(dab[:, :256], wg[c:c + 512, :]) + nt(dab[:, 256:], wu[c:c + 512, :])
        ip[:, :, c:c + 512] = part.astype(BF).reshape(dyin.shape[0], SLAB, 512)
    ip[:, :, width:] = jnp.broadcast_to(gate_part, (rows, LANES)).reshape(dyin.shape[0], SLAB, LANES)
    back = [[], []]
    for k, hh in enumerate((1 - h, h)):
        for d in range(1, nx):
            back[k].append(send(ip.at[lax.rem(x + d, nx) * NH + hh], ret.at[x, k], x_dev(d)))
        ret[x, k] = ip[x * NH + hh]

    def pass_on(k):
        up[k].wait_recv()
        down[k].wait_recv()
        if k < 2:
            up.append(send(gp_in.at[k], gp_in.at[k + 1], y_dev(1)))
            down.append(send(gm_in.at[k], gm_in.at[k + 1], y_dev(NY - 1)))
        else:
            up.append(send(gp_in.at[k, pl.ds(0, hr)], g4_in.at[pl.ds(0, hr)], y_dev(1)))
            down.append(send(gm_in.at[k, pl.ds(hr, hr)], g4_in.at[pl.ds(hr, hr)], y_dev(NY - 1)))

    pad_n = jnp.zeros((LANES - n_rows, 512), BF)

    def wide(ref_val):
        return jnp.concatenate([ref_val, pad_n], axis=0)

    pass_on(0)

    for b in range(nz):
        dyt[b] = dyin[:, :, b * zw:(b + 1) * zw].reshape(rows, zw).T
    order = [4, 3, 5, 2, 6, 1, 7, 0]
    chip = {}

    def down_part(d):
        yt = lax.rem(y + d, NY)
        lo = pl.multiple_of(yt * yw + (1 - core) * cw, cw)
        part = nn(dyt[:, pl.ds(lo, cw), :].reshape(nz * cw, LANES), hg[...])
        gds[d] = part.astype(BF)
        chip[d] = send(gds.at[d], gdr.at[d], c_dev)
        lo = pl.multiple_of(yt * yw + core * cw, cw)
        gdo[d] = nn(dyt[:, pl.ds(lo, cw), :].reshape(nz * cw, LANES), hg[...])

    for d in order[:4]:
        down_part(d)
    pass_on(1)
    for d in order[4:]:
        down_part(d)

    def chip_sum(d):
        chip[d].wait_recv()
        return gdo[d] + gdr[d].astype(F32)

    far = chip_sum(4).astype(BF)
    psend[0] = far
    p_in = [send(psend.at[0, pl.ds(0, half)], p0r, y_dev(1))]
    m_in = [send(psend.at[0, pl.ds(half, half)], m0r, y_dev(NY - 1))]

    lo = pl.multiple_of(y * yw, yw)
    acc = nn(xt[:, pl.ds(lo, yw), :].reshape(nz * yw, LANES), wide(nar[...]))
    gx[...] = acc.reshape(nz, yw, 512)

    def add_factor(d, value):
        x_in[d - 1].wait_recv()
        part = nn(xty[d - 1].reshape(nz * yw, LANES), wide(value))
        gx[...] = gx[...] + part.reshape(nz, yw, 512)

    pass_on(2)
    add_factor(1, gp_in[0])
    add_factor(NY - 1, gm_in[0])

    for copy in back[0]:
        copy.wait_recv()
    for e in range(2):
        zsum[e * SLAB:(e + 1) * SLAB] = (
            ret[2 * e, 0].astype(F32) + ret[2 * e + 1, 0].astype(F32)).astype(BF)
    z_back = send(zsum, zrin, h_dev)

    p_in[0].wait_recv()
    s3 = chip_sum(3)
    psend[1, 0:half] = (s3[0:half] + p0r[...].astype(F32)).astype(BF)
    psend[1, half:] = s3[half:].astype(BF)
    p_in.append(send(psend.at[1], prr.at[0], y_dev(1)))
    m_in[0].wait_recv()
    s5 = chip_sum(5)
    msend[0, 0:half] = s5[0:half].astype(BF)
    msend[0, half:] = (s5[half:] + m0r[...].astype(F32)).astype(BF)
    m_in.append(send(msend.at[0], mrr.at[0], y_dev(NY - 1)))
    add_factor(2, gp_in[1])
    add_factor(NY - 2, gm_in[1])
    add_factor(3, gp_in[2])
    add_factor(NY - 3, gm_in[2])
    p_in[1].wait_recv()
    psend[2] = (chip_sum(2) + prr[0].astype(F32)).astype(BF)
    p_in.append(send(psend.at[2], prr.at[1], y_dev(1)))
    m_in[1].wait_recv()
    msend[1] = (chip_sum(6) + mrr[0].astype(F32)).astype(BF)
    m_in.append(send(msend.at[1], mrr.at[1], y_dev(NY - 1)))
    up[3].wait_recv()
    down[3].wait_recv()
    add_factor(4, g4_in[...])
    lo = pl.multiple_of((1 - core) * cw, cw)
    x_chip = send(gx.at[:, pl.ds(lo, cw), :], gxr, c_dev)
    p_in[2].wait_recv()
    psend[3] = (chip_sum(1) + prr[1].astype(F32)).astype(BF)
    p_in.append(send(psend.at[3], prr.at[2], y_dev(1)))
    m_in[2].wait_recv()
    msend[2] = (chip_sum(7) + mrr[1].astype(F32)).astype(BF)
    m_in.append(send(msend.at[2], mrr.at[2], y_dev(NY - 1)))

    x_chip.wait_recv()
    lo = pl.multiple_of(core * cw, cw)
    sx[...] = gx[:, pl.ds(lo, cw), :] + gxr[...]
    zx_in = []
    for d in range(1, nz):
        zsx[d - 1] = sx[lax.rem(z + d, nz)].astype(BF)
        zx_in.append(send(zsx.at[d - 1], zrx.at[d - 1], z_dev(d)))

    for copy in back[1]:
        copy.wait_recv()
    z_back.wait_recv()
    out = []
    tops, lows = [], []
    for e in range(2):
        total = (ret[2 * e, 1].astype(F32) + ret[2 * e + 1, 1].astype(F32)
                 + zrin[e * SLAB:(e + 1) * SLAB].astype(F32))
        high = total.astype(BF)
        tops.append(high)
        lows.append((total - high.astype(F32)).astype(BF))
        gs2 = total[:, width:]
        gs2 = jnp.concatenate([gs2, gs2], axis=1)
        out.append(jnp.sum(pl_ref[e * SLAB:(e + 1) * SLAB] * gs2, axis=0, keepdims=True))
    gg_ref[0:1] = jnp.where(r0 == 0, out[0], 0.0) + jnp.where(r0 == 1, out[1], 0.0)
    gg_ref[1:2] = jnp.where(r1 == 0, out[0], 0.0) + jnp.where(r1 == 1, out[1], 0.0)
    both = jnp.concatenate(
        tops + lows + [jnp.zeros((LANES - 4 * SLAB, width + LANES), BF)], axis=0)
    stores = []
    for i, c in enumerate(range(0, width, 1024)):
        for c2 in range(c, c + 1024, 512):
            ig[:, c2:c2 + 512] = nn(plt_ref[...], both[:, c2:c2 + 512]).astype(BF)
        store = pltpu.make_async_copy(
            ig.at[:, pl.ds(c, 1024)], ig_hbm.at[:, pl.ds(c, 1024)], loc_sem.at[5 + i])
        store.start()
        stores.append(store)

    p_in[3].wait_recv()
    m_in[3].wait_recv()
    total = chip_sum(0) + prr[2].astype(F32) + mrr[2].astype(F32)
    sd[...] = total.reshape(nz, cw, 256)
    zd_in = []
    for d in range(1, nz):
        zsd[d - 1] = sd[lax.rem(z + d, nz)].astype(BF)
        zd_in.append(send(zsd.at[d - 1], zrd.at[d - 1], z_dev(d)))
    acc = sx[z]
    for d in range(1, nz):
        zx_in[d - 1].wait_recv()
        acc = acc + zrx[d - 1].astype(F32)
    wgr_ref[0] = acc[:, :256]
    wgr_ref[1] = acc[:, 256:]
    acc = sd[z]
    for d in range(1, nz):
        zd_in[d - 1].wait_recv()
        acc = acc + zrd[d - 1].astype(F32)
    wgr_ref[2] = acc
    for store in stores:
        store.wait()
    for copy in started:
        copy.wait_send()


def per_device(grad_out, routes, gate_levels, saved_inputs, w_gate, w_up, w_down):
    group, n_dp = lax.axis_size("expert"), lax.axis_size("dp")
    nx, nz = group // NH, n_dp // (NY * NC)
    n_rows, width = saved_inputs.shape
    cap = n_rows // group
    toks = grad_out.shape[0]
    f = w_gate.shape[1]
    rows = group * SLAB
    ext = width + LANES
    zw = width // nz
    yw = zw // NY
    cw = yw // NC
    own = nz * cw
    V = pltpu.VMEM
    scratch = [
        V((toks, width), BF), V((n_rows, width), BF), V((width, f), BF), V((width, f), BF),
        V((f, width), BF), V((toks, width), BF),
        V((2 * SLAB, toks), F32), V((toks, LANES), BF), V((2 * SLAB, ext), BF),
        V((2 * SLAB, ext), BF), V((group, SLAB, ext), BF), V((rows, width), BF),
        V((nz, zw, LANES), BF), V((NY - 1, nz, yw, LANES), BF),
        V((rows, f), F32), V((rows, f), F32), V((rows, f), F32),
        V((n_rows, 2 * f), BF), V((3, n_rows, 2 * f), BF), V((3, n_rows, 2 * f), BF),
        V((n_rows, 2 * f), BF), V((rows, 2 * f), BF), V((rows, f), BF),
        V((group, SLAB, ext), BF), V((nx, 2, SLAB, ext), BF), V((2 * SLAB, ext), BF),
        V((2 * SLAB, ext), BF), V((nz, zw, LANES), BF),
        V((NY, own, f), BF), V((NY, own, f), BF), V((NY, own, f), F32),
        V((4, own, f), BF), V((3, own, f), BF), V((3, own, f), BF), V((3, own, f), BF),
        V((own // 2, f), BF), V((own // 2, f), BF), V((nz, cw, f), F32),
        V((nz, yw, 2 * f), F32), V((nz, cw, 2 * f), F32), V((nz, cw, 2 * f), F32),
        V((nz - 1, cw, f), BF), V((nz - 1, cw, f), BF),
        V((nz - 1, cw, 2 * f), BF), V((nz - 1, cw, 2 * f), BF),
        pltpu.SemaphoreType.DMA((8,)), pltpu.SemaphoreType.DMA((80,)),
        pltpu.SemaphoreType.DMA((80,)),
    ]
    vm = pl.BlockSpec(memory_space=pltpu.VMEM)
    anywhere = pl.BlockSpec(memory_space=pl.ANY)
    input_grad, gate_grad, weight_grad = pl.pallas_call(
        functools.partial(kernel, nx, nz, cap),
        out_shape=[
            jax.ShapeDtypeStruct((toks, width), BF),
            jax.ShapeDtypeStruct((2, toks), F32),
            jax.ShapeDtypeStruct((3, cw, f), F32),
        ],
        in_specs=[vm, vm] + [anywhere] * 5,
        out_specs=[anywhere, vm, vm],
        scratch_shapes=scratch,
        compiler_params=pltpu.CompilerParams(
            collective_id=0, has_side_effects=True, vmem_limit_bytes=56 * 1024 * 1024),
    )(routes.T, gate_levels.T, grad_out, saved_inputs, w_gate, w_up, w_down)
    return (input_grad, gate_grad.T, jnp.transpose(weight_grad, (1, 0, 2)))


def solution(mesh):
    in_specs = (
        P(("dp", "expert"), None),
        P(("dp", "expert"), None),
        P(("dp", "expert"), None),
        P(("dp", "expert"), None),
        P(None, "expert"),
        P(None, "expert"),
        P("expert", None),
    )
    out_specs = (P(("dp", "expert"), None), P(("dp", "expert"), None), P("dp", None, "expert"))
    return jax.shard_map(
        per_device, mesh=mesh, in_specs=in_specs, out_specs=out_specs, check_vma=False
    )
```

time: 1790 us -> 85.6 us (0.05)
  the two profiles are of different devices: /device:TPU:1 before, /device:TPU:24 now
where the time goes in v1:
time: 85.6 us; the launch traced here: 85.4 us
  Pallas kernels  80.8 us (94%)
  local copies, waits for them, and re-layouts  3.91 us (5%)
    pallas_call x1, Pallas kernels, per_device(): pl.pallas_call(functools.partial(kernel, nx, nz, cap), out_shape=[jax.Sha...  80.8 us
    unnamed x7, local copies, waits for them, and re-layouts  3.91 us

profile of v1, /device:TPU:24, one launch (start us, length us, event | category | flops | bytes accessed | tf_op | source)
XLA Modules:
  0.0 85.4 jit_solution(12879870706445825306)
XLA Ops:
  0.6 80.8 %shard_map.94 = (bf16[256,3072]{1,0:T(8,128)(2,1)}, f32[2,256]{1,0:T(2,128)}, f32[3,32,256]{2,1,0:T(8,128)}) custom-call(s32[2,256]{1,0:T(2,128)} %bitcast.5, s32[2,256]{1,0:T(2,128)} %bitcast.6, bf16[256,3072]{1,0:T(8,128)(2,1)} %go_hbm.1, bf16[96,3072]{1,0:T(8,128)(2,1)} %x_hbm.1, bf16[3072,256]{1,0:T(8,128)(2,1)} %wg_hbm.1, bf16[3072,256]{1,0:T(8,128)(2,1)} %wu_hbm.1, ...), custom_call_target="tpu_custom_call" | custom-call | tf_op jit(solution)/shard_map/pallas_call | solution.py:397
  81.5 0.0 copy-start.1
  81.5 0.0 copy-start
  81.5 2.7 %copy.13 = bf16[256,3072]{1,0:T(8,128)(2,1)} copy(bf16[256,3072]{1,0:T(8,128)(2,1)} %get-tuple-element.12) | data formatting | bytes 3145728
  84.2 0.0 copy-done.1
  84.2 0.6 copy.14
  84.8 0.0 copy-done
  84.8 0.6 copy.15
Async XLA Ops:
  81.5 2.7 %copy-start.1 = (f32[2,256]{1,0:T(2,128)S(1)}, f32[2,256]{1,0:T(2,128)}, u32[]{:S(2)}) copy-start(f32[2,256]{1,0:T(2,128)} %get-tuple-element.7) | copy-start | bytes 6148
  81.5 3.3 %copy-start = (f32[3,32,256]{2,1,0:T(8,128)S(1)}, f32[3,32,256]{2,1,0:T(8,128)}, u32[]{:S(2)}) copy-start(f32[3,32,256]{2,1,0:T(8,128)} %get-tuple-element.8) | copy-start | bytes 294916

commit v2 on v1

v2 whole, which is shorter than its diff:
```python
import functools

import jax
import jax.numpy as jnp
from jax import lax
from jax.experimental import pallas as pl
from jax.experimental.pallas import tpu as pltpu
from jax.sharding import PartitionSpec as P

NY, NC, NH = 8, 2, 2
SLAB = 16
LANES = 128
BF, F32 = jnp.bfloat16, jnp.float32


def nt(a, b):
    return lax.dot_general(a, b, (((1,), (1,)), ((), ())), preferred_element_type=F32)


def nn(a, b):
    return lax.dot_general(a, b, (((1,), (0,)), ((), ())), preferred_element_type=F32)


def kernel(
    nx, nz, cap,
    routes_ref, levels_ref, go_hbm, x_hbm, wg_hbm, wu_hbm, wd_hbm,
    both_ref, plt_ref, gg_ref, wgr_ref,
    go, xv, wg, wu, wd,
    pl_ref, pk, pkx, zin, zinx, dyin, xp, xs, xty, act, hid, dfac,
    nar, gp_in, gm_in, g4_in, dab, hg, ip, ret, zsum, zrin, dyt,
    gds, gdr, gdo, psend, prr, msend, mrr, p0r, m0r, sd, gx, gxr, sx,
    zsd, zrd, zsx, zrx, loc_sem, send_sem, recv_sem,
):
    dp, ex = lax.axis_index("dp"), lax.axis_index("expert")
    core = lax.rem(dp, NC)
    y = lax.rem(lax.div(dp, NC), NY)
    z = lax.div(dp, NC * NY)
    h = lax.rem(ex, NH)
    x = lax.div(ex, NH)
    width = go.shape[1]
    rows = dyin.shape[0] * SLAB
    zw = width // nz
    yw = zw // NY
    cw = yw // NC
    half = nz * cw // 2

    def x_dev(d):
        return (dp, lax.rem(x + d, nx) * NH + h)

    h_dev = (dp, x * NH + (1 - h))

    def y_dev(d):
        return ((z * NY + lax.rem(y + d, NY)) * NC + core, ex)

    c_dev = ((z * NY + y) * NC + (1 - core), ex)

    def z_dev(d):
        return ((lax.rem(z + d, nz) * NY + y) * NC + core, ex)

    started = []

    def send(src, dst, dev):
        i = len(started)
        copy = pltpu.make_async_remote_copy(
            src_ref=src, dst_ref=dst, send_sem=send_sem.at[i], recv_sem=recv_sem.at[i],
            device_id=dev, device_id_type=pl.DeviceIdType.MESH,
        )
        copy.start()
        started.append(copy)
        return copy

    quarter = width // 4
    cols = [(k * quarter, quarter + (LANES if k == 3 else 0)) for k in range(4)]
    go_loads = [
        pltpu.make_async_copy(
            go_hbm.at[:, pl.ds(a, quarter)], go.at[:, pl.ds(a, quarter)], loc_sem.at[4 + k])
        for k, (a, _) in enumerate(cols)
    ]
    loads = [
        pltpu.make_async_copy(src, dst, loc_sem.at[i])
        for i, (src, dst) in enumerate([(x_hbm, xv), (wg_hbm, wg), (wu_hbm, wu), (wd_hbm, wd)])
    ]
    for load in go_loads:
        load.start()
    loads[0].start()
    barrier = pltpu.get_barrier_semaphore()
    partners = (
        [h_dev] + [x_dev(d) for d in range(1, nx)] + [y_dev(d) for d in range(1, NY)]
        + [c_dev] + [z_dev(d) for d in range(1, nz)]
    )
    for dev in partners:
        pl.semaphore_signal(barrier, inc=1, device_id=dev, device_id_type=pl.DeviceIdType.MESH)

    toks = go.shape[0]
    r = routes_ref[...]
    lv = levels_ref[...].astype(F32)
    r0, r1, l0, l1 = r[0:1], r[1:2], lv[0:1], lv[1:2]
    mem = [jnp.where((r0 == e) | (r1 == e), 1.0, 0.0) for e in range(2)]
    lev = [jnp.where(r0 == e, l0, 0.0) + jnp.where(r1 == e, l1, 0.0) for e in range(2)]
    row8 = lax.broadcasted_iota(jnp.int32, (8, toks), 0)
    m8 = jnp.where(row8 == 0, mem[0], jnp.where(row8 == 1, mem[1], 0.0)).astype(BF)
    tri = jnp.where(
        lax.broadcasted_iota(jnp.int32, (toks, toks), 0)
        <= lax.broadcasted_iota(jnp.int32, (toks, toks), 1), 1.0, 0.0,
    ).astype(BF)
    slots = nn(m8, tri) - 1.0
    row = lax.broadcasted_iota(jnp.int32, (2 * cap, toks), 0)
    first = row < cap
    want = jnp.where(first, row, row - cap).astype(F32)
    slot_row = jnp.where(first, slots[0:1], slots[1:2])
    mem_row = jnp.where(first, mem[0], mem[1])
    lev_row = jnp.where(first, lev[0], lev[1])
    placed = jnp.where((mem_row > 0.5) & (slot_row == want), 1.0, 0.0)
    pl_ref[...] = placed
    gate = jnp.sum(placed * lev_row, axis=1, keepdims=True) * (1.0 / 16.0)
    pk[:, width:] = jnp.broadcast_to(gate, (2 * cap, LANES)).astype(BF)
    placed_b = placed.astype(BF)

    ei = lax.broadcasted_iota(jnp.int32, (2 * SLAB, 2 * cap), 0)
    ek = lax.broadcasted_iota(jnp.int32, (2 * SLAB, 2 * cap), 1)
    ec = jnp.bitwise_and(ei, SLAB - 1)
    expand = jnp.where(
        (ec < cap) & (ek == jnp.right_shift(ei, 4) * cap + ec), 1.0, 0.0).astype(BF)
    ci = lax.broadcasted_iota(jnp.int32, (2 * cap, nx * SLAB), 0)
    ck = lax.broadcasted_iota(jnp.int32, (2 * cap, nx * SLAB), 1)
    ce = jnp.where(ck < nx * SLAB // 2, 0, 1)
    compact = jnp.where(
        ci == ce * cap + jnp.bitwise_and(ck, SLAB - 1), 1.0, 0.0)
    compact = jnp.where(jnp.bitwise_and(ck, SLAB - 1) < cap, compact, 0.0).astype(BF)

    mine, other = x * NH + h, x * NH + (1 - h)
    z_in = []
    for k, (a, w) in enumerate(cols):
        go_loads[k].wait()
        pk[:, a:a + quarter] = nn(placed_b, go[:, a:a + quarter]).astype(BF)
        if k == 0:
            pl.semaphore_wait(barrier, len(partners))
        z_in.append(send(pk.at[:, pl.ds(a, w)], zin.at[:, pl.ds(a, w)], h_dev))
    for load in loads[1:]:
        load.start()

    loads[0].wait()
    n_rows = xv.shape[0]
    for t in range(NY):
        for b in range(0, nz, 2):
            lo = b * zw + t * yw
            xs[t, :, b * yw:(b + 2) * yw] = jnp.concatenate(
                [xv[:, lo:lo + yw], xv[:, lo + zw:lo + zw + yw]], axis=1)
    x_in = []
    for d in range(1, NY):
        x_in.append(send(xs.at[lax.rem(y + d, NY)], xty.at[d - 1], y_dev(d)))

    def spread(src, slab, a, w):
        got = []
        for d in range(1, nx):
            e = lax.div(lax.rem(x + d, nx), nx // 2)
            lo = pl.multiple_of(e * SLAB, SLAB)
            got.append(send(src.at[pl.ds(lo, SLAB), pl.ds(a, w)],
                            dyin.at[slab, :, pl.ds(a, w)], x_dev(d)))
        return got

    own = pl.multiple_of(lax.div(x, nx // 2) * SLAB, SLAB)
    for a, w in cols:
        pkx[:, a:a + w] = nn(expand, pk[:, a:a + w]).astype(BF)
    dy_own = spread(pkx, mine, 0, width + LANES)
    dyin[mine] = pkx[pl.ds(own, SLAB), :]

    gi = lax.broadcasted_iota(jnp.int32, (rows, n_rows), 0)
    gk = lax.broadcasted_iota(jnp.int32, (rows, n_rows), 1)
    gc = jnp.bitwise_and(gi, SLAB - 1)
    gs = jnp.right_shift(gi, 4)
    widen = jnp.where((gc < cap) & (gk == gs * cap + gc), 1.0, 0.0).astype(BF)
    ni = lax.broadcasted_iota(jnp.int32, (n_rows, rows), 0)
    nk = lax.broadcasted_iota(jnp.int32, (n_rows, rows), 1)
    nc_ = jnp.bitwise_and(nk, SLAB - 1)
    ns = jnp.right_shift(nk, 4)
    narrow = jnp.where((nc_ < cap) & (ni == ns * cap + nc_), 1.0, 0.0).astype(BF)
    for c in range(0, width, 512):
        xp[:, c:c + 512] = nn(widen, xv[:, c:c + 512]).astype(BF)
    loads[1].wait()
    a_pre = nn(xp[...], wg[...])
    loads[2].wait()
    b_pre = nn(xp[...], wu[...])
    sigma = jax.nn.sigmoid(a_pre)
    activ = a_pre * sigma
    act[...] = activ
    hid[...] = activ * b_pre
    dfac[...] = b_pre * sigma * (1.0 + a_pre * (1.0 - sigma))
    pl_two = jnp.concatenate(
        [pl_ref[...], pl_ref[...], jnp.zeros((LANES - 4 * cap, toks), F32)], axis=0)
    plt_ref[...] = pl_two.T[:, :4 * cap].astype(BF)

    loads[3].wait()
    dy_other = []
    for k, (a, w) in enumerate(cols):
        z_in[k].wait_recv()
        zinx[:, a:a + w] = nn(expand, zin[:, a:a + w]).astype(BF)
        dy_other.append(spread(zinx, other, a, w))
    dyin[other] = zinx[pl.ds(own, SLAB), :]
    for copy in dy_own:
        copy.wait_recv()
    proj = jnp.zeros((rows, wd.shape[0]), F32)
    for k, (a, w) in enumerate(cols):
        for copy in dy_other[k]:
            copy.wait_recv()
        proj += nt(dyin[:, :, a:a + quarter].reshape(rows, quarter), wd[:, a:a + quarter])
    g_half = dyin[:, :, width:].reshape(rows, LANES).astype(F32)
    g = jnp.concatenate([g_half, g_half], axis=1)
    d_hid = g * proj
    dab[:, 256:] = (d_hid * act[...]).astype(BF)
    dab[:, :256] = (d_hid * dfac[...]).astype(BF)
    hg[...] = (g * hid[...]).astype(BF)
    gate_part = jnp.sum(hid[...] * proj, axis=1, keepdims=True).astype(BF)

    f = hg.shape[1]
    both_parts = nn(narrow, dab[...]).astype(BF)
    hr = n_rows // 2
    up, down = [], []
    for i in range(2):
        nar[i] = both_parts[:, i * f:(i + 1) * f]
        up.append([send(nar.at[i], gp_in.at[0, i], y_dev(1))])
        down.append([send(nar.at[i], gm_in.at[0, i], y_dev(NY - 1))])

    ip[:, :, width:] = jnp.broadcast_to(gate_part, (rows, LANES)).reshape(dyin.shape[0], SLAB, LANES)
    halves = [(0, width // 2), (width // 2, width // 2 + LANES)]
    back = [[], [], []]
    for k, (a, w) in enumerate(halves):
        for c in range(a, a + width // 2, 512):
            part = nt(dab[:, :256], wg[c:c + 512, :]) + nt(dab[:, 256:], wu[c:c + 512, :])
            ip[:, :, c:c + 512] = part.astype(BF).reshape(dyin.shape[0], SLAB, 512)
        for d in range(1, nx):
            back[k].append(send(ip.at[lax.rem(x + d, nx) * NH + 1 - h, :, pl.ds(a, w)],
                                ret.at[0, x, :, pl.ds(a, w)], x_dev(d)))
    for d in range(1, nx):
        back[2].append(send(ip.at[lax.rem(x + d, nx) * NH + h], ret.at[1, x], x_dev(d)))
    ret[0, x] = ip[x * NH + 1 - h]
    ret[1, x] = ip[x * NH + h]

    def pass_on(k):
        for i in range(2):
            up[i][k].wait_recv()
            if k < 2:
                up[i].append(send(gp_in.at[k, i], gp_in.at[k + 1, i], y_dev(1)))
            else:
                up[i].append(send(gp_in.at[k, i, pl.ds(0, hr)], g4_in.at[i, pl.ds(0, hr)], y_dev(1)))
            down[i][k].wait_recv()
            if k < 2:
                down[i].append(send(gm_in.at[k, i], gm_in.at[k + 1, i], y_dev(NY - 1)))
            else:
                down[i].append(send(
                    gm_in.at[k, i, pl.ds(hr, hr)], g4_in.at[i, pl.ds(hr, hr)], y_dev(NY - 1)))

    pad_n = jnp.zeros((LANES - n_rows, 512), BF)
    pad_x = jnp.zeros((LANES - n_rows, nz * yw), BF)

    def factor(cut, value):
        value = jnp.concatenate([value[0], value[1]], axis=1)
        return nn(jnp.concatenate([cut, pad_x], axis=0).T, jnp.concatenate([value, pad_n], axis=0))

    for b in range(nz):
        dyt[b] = dyin[:, :, b * zw:(b + 1) * zw].reshape(rows, zw).T
    chip = {}

    def down_part(d):
        yt = lax.rem(y + d, NY)
        lo = pl.multiple_of(yt * yw + (1 - core) * cw, cw)
        part = nn(dyt[:, pl.ds(lo, cw), :].reshape(nz * cw, LANES), hg[...])
        gds[d] = part.astype(BF)
        chip[d] = send(gds.at[d], gdr.at[d], c_dev)
        lo = pl.multiple_of(yt * yw + core * cw, cw)
        gdo[d] = nn(dyt[:, pl.ds(lo, cw), :].reshape(nz * cw, LANES), hg[...])

    def chip_sum(d):
        chip[d].wait_recv()
        return gdo[d] + gdr[d].astype(F32)

    for d in (4, 3, 5, 2):
        down_part(d)
    pass_on(0)
    psend[0] = chip_sum(4).astype(BF)
    p_in = [send(psend.at[0, pl.ds(0, half)], p0r, y_dev(1))]
    m_in = [send(psend.at[0, pl.ds(half, half)], m0r, y_dev(NY - 1))]
    for d in (6, 1, 7, 0):
        down_part(d)
    gx[...] = factor(xs[y], nar[...]).reshape(nz, yw, 2 * f)

    def add_factor(d, value):
        x_in[d - 1].wait_recv()
        gx[...] = gx[...] + factor(xty[d - 1], value).reshape(nz, yw, 2 * f)

    z_back = []

    def cross(k):
        a, w = halves[k]
        for copy in back[k]:
            copy.wait_recv()
        zsum[:, a:a + w] = nn(compact, ret[0, :, :, a:a + w].reshape(nx * SLAB, w)).astype(BF)
        z_back.append(send(zsum.at[:, pl.ds(a, w)], zrin.at[:, pl.ds(a, w)], h_dev))

    cross(0)
    pass_on(1)
    cross(1)
    p_in[0].wait_recv()
    s3 = chip_sum(3)
    psend[1, 0:half] = (s3[0:half] + p0r[...].astype(F32)).astype(BF)
    psend[1, half:] = s3[half:].astype(BF)
    p_in.append(send(psend.at[1], prr.at[0], y_dev(1)))
    m_in[0].wait_recv()
    s5 = chip_sum(5)
    msend[0, 0:half] = s5[0:half].astype(BF)
    msend[0, half:] = (s5[half:] + m0r[...].astype(F32)).astype(BF)
    m_in.append(send(msend.at[0], mrr.at[0], y_dev(NY - 1)))
    add_factor(1, gp_in[0])
    add_factor(NY - 1, gm_in[0])
    pass_on(2)
    add_factor(2, gp_in[1])
    add_factor(NY - 2, gm_in[1])
    p_in[1].wait_recv()
    psend[2] = (chip_sum(2) + prr[0].astype(F32)).astype(BF)
    p_in.append(send(psend.at[2], prr.at[1], y_dev(1)))
    m_in[1].wait_recv()
    msend[1] = (chip_sum(6) + mrr[0].astype(F32)).astype(BF)
    m_in.append(send(msend.at[1], mrr.at[1], y_dev(NY - 1)))
    add_factor(3, gp_in[2])
    add_factor(NY - 3, gm_in[2])
    for i in range(2):
        up[i][3].wait_recv()
        down[i][3].wait_recv()
    add_factor(4, g4_in[...])
    lo = pl.multiple_of((1 - core) * cw, cw)
    x_chip = send(gx.at[:, pl.ds(lo, cw), :], gxr, c_dev)
    x_chip.wait_recv()
    lo = pl.multiple_of(core * cw, cw)
    sx[...] = gx[:, pl.ds(lo, cw), :] + gxr[...]
    zx_in = []
    for d in range(1, nz):
        zsx[d - 1] = sx[lax.rem(z + d, nz)].astype(BF)
        zx_in.append(send(zsx.at[d - 1], zrx.at[d - 1], z_dev(d)))

    p_in[2].wait_recv()
    psend[3] = (chip_sum(1) + prr[1].astype(F32)).astype(BF)
    p_in.append(send(psend.at[3], prr.at[2], y_dev(1)))
    m_in[2].wait_recv()
    msend[2] = (chip_sum(7) + mrr[1].astype(F32)).astype(BF)
    m_in.append(send(msend.at[2], mrr.at[2], y_dev(NY - 1)))
    p_in[3].wait_recv()
    m_in[3].wait_recv()
    total = chip_sum(0) + prr[2].astype(F32) + mrr[2].astype(F32)
    sd[...] = total.reshape(nz, cw, 256)
    zd_in = []
    for d in range(1, nz):
        zsd[d - 1] = sd[lax.rem(z + d, nz)].astype(BF)
        zd_in.append(send(zsd.at[d - 1], zrd.at[d - 1], z_dev(d)))

    for copy in back[2]:
        copy.wait_recv()
    for k, (a, w) in enumerate(halves):
        z_back[k].wait_recv()
        total = (nn(compact, ret[1, :, :, a:a + w].reshape(nx * SLAB, w))
                 + zrin[:, a:a + w].astype(F32))
        n = width // 2
        high = total[:, :n].astype(BF)
        both_ref[0:2 * cap, a:a + n] = high
        both_ref[2 * cap:, a:a + n] = (total[:, :n] - high.astype(F32)).astype(BF)
    gs2 = total[:, n:]
    prod = pl_ref[...] * jnp.concatenate([gs2, gs2], axis=1)
    top = lax.broadcasted_iota(jnp.int32, (2 * cap, toks), 0) < cap
    out = [jnp.sum(jnp.where(top, prod, 0.0), axis=0, keepdims=True),
           jnp.sum(jnp.where(top, 0.0, prod), axis=0, keepdims=True)]
    gg_ref[0:1] = jnp.where(r0 == 0, out[0], 0.0) + jnp.where(r0 == 1, out[1], 0.0)
    gg_ref[1:2] = jnp.where(r1 == 0, out[0], 0.0) + jnp.where(r1 == 1, out[1], 0.0)

    acc = sx[z]
    for d in range(1, nz):
        zx_in[d - 1].wait_recv()
        acc = acc + zrx[d - 1].astype(F32)
    wgr_ref[0] = acc[:, :256]
    wgr_ref[1] = acc[:, 256:]
    acc = sd[z]
    for d in range(1, nz):
        zd_in[d - 1].wait_recv()
        acc = acc + zrd[d - 1].astype(F32)
    wgr_ref[2] = acc
    for copy in started:
        copy.wait_send()


def finish(spots_hbm, both_hbm, gg_hbm, wgr_hbm, ig_hbm, gg_out, wgr_out,
           spots, both, ig, gg, wgr, sem):
    width, cut = ig.shape[1], 512
    parts = range(0, width, cut)
    first = pltpu.make_async_copy(spots_hbm, spots, sem.at[0])
    first.start()
    gets = [pltpu.make_async_copy(both_hbm.at[:, pl.ds(c, cut)], both.at[:, pl.ds(c, cut)],
                                  sem.at[5 + i]) for i, c in enumerate(parts)]
    for get in gets:
        get.start()
    get_g = pltpu.make_async_copy(gg_hbm, gg, sem.at[1])
    get_w = pltpu.make_async_copy(wgr_hbm, wgr, sem.at[2])
    get_g.start()
    get_w.start()
    first.wait()
    puts = []
    for i, c in enumerate(parts):
        gets[i].wait()
        ig[:, c:c + cut] = nn(spots[...], both[:, c:c + cut]).astype(BF)
        put = pltpu.make_async_copy(
            ig.at[:, pl.ds(c, cut)], ig_hbm.at[:, pl.ds(c, cut)], sem.at[5 + len(parts) + i])
        put.start()
        puts.append(put)
    get_g.wait()
    get_w.wait()
    puts.append(pltpu.make_async_copy(gg, gg_out, sem.at[3]))
    puts.append(pltpu.make_async_copy(wgr, wgr_out, sem.at[4]))
    for put in puts[-2:]:
        put.start()
    for put in puts:
        put.wait()


def per_device(grad_out, routes, gate_levels, saved_inputs, w_gate, w_up, w_down):
    group, n_dp = lax.axis_size("expert"), lax.axis_size("dp")
    nx, nz = group // NH, n_dp // (NY * NC)
    n_rows, width = saved_inputs.shape
    cap = n_rows // group
    toks = grad_out.shape[0]
    f = w_gate.shape[1]
    rows = group * SLAB
    ext = width + LANES
    zw = width // nz
    yw = zw // NY
    cw = yw // NC
    own = nz * cw
    V = pltpu.VMEM
    scratch = [
        V((toks, width), BF), V((n_rows, width), BF), V((width, f), BF), V((width, f), BF),
        V((f, width), BF),
        V((2 * cap, toks), F32), V((2 * cap, ext), BF), V((2 * SLAB, ext), BF),
        V((2 * cap, ext), BF), V((2 * SLAB, ext), BF), V((group, SLAB, ext), BF),
        V((rows, width), BF),
        V((NY, n_rows, nz * yw), BF), V((NY - 1, n_rows, nz * yw), BF),
        V((rows, f), F32), V((rows, f), F32), V((rows, f), F32),
        V((2, n_rows, f), BF), V((3, 2, n_rows, f), BF), V((3, 2, n_rows, f), BF),
        V((2, n_rows, f), BF), V((rows, 2 * f), BF), V((rows, f), BF),
        V((group, SLAB, ext), BF), V((2, nx, SLAB, ext), BF), V((2 * cap, ext), BF),
        V((2 * cap, ext), BF), V((nz, zw, LANES), BF),
        V((NY, own, f), BF), V((NY, own, f), BF), V((NY, own, f), F32),
        V((4, own, f), BF), V((3, own, f), BF), V((3, own, f), BF), V((3, own, f), BF),
        V((own // 2, f), BF), V((own // 2, f), BF), V((nz, cw, f), F32),
        V((nz, yw, 2 * f), F32), V((nz, cw, 2 * f), F32), V((nz, cw, 2 * f), F32),
        V((nz - 1, cw, f), BF), V((nz - 1, cw, f), BF),
        V((nz - 1, cw, 2 * f), BF), V((nz - 1, cw, 2 * f), BF),
        pltpu.SemaphoreType.DMA((8,)), pltpu.SemaphoreType.DMA((100,)),
        pltpu.SemaphoreType.DMA((100,)),
    ]
    vm = pl.BlockSpec(memory_space=pltpu.VMEM)
    anywhere = pl.BlockSpec(memory_space=pl.ANY)
    both, spots, gate_grad, weight_grad = pl.pallas_call(
        functools.partial(kernel, nx, nz, cap),
        out_shape=[
            jax.ShapeDtypeStruct((4 * cap, width), BF),
            jax.ShapeDtypeStruct((toks, 4 * cap), BF),
            jax.ShapeDtypeStruct((2, toks), F32),
            jax.ShapeDtypeStruct((3, cw, f), F32),
        ],
        in_specs=[vm, vm] + [anywhere] * 5,
        out_specs=[vm, vm, vm, vm],
        scratch_shapes=scratch,
        compiler_params=pltpu.CompilerParams(
            collective_id=0, has_side_effects=True, vmem_limit_bytes=56 * 1024 * 1024),
    )(routes.T, gate_levels.T, grad_out, saved_inputs, w_gate, w_up, w_down)
    input_grad, gate_grad, weight_grad = pl.pallas_call(
        finish,
        out_shape=[
            jax.ShapeDtypeStruct((toks, width), BF),
            jax.ShapeDtypeStruct((2, toks), F32),
            jax.ShapeDtypeStruct((3, cw, f), F32),
        ],
        in_specs=[anywhere] * 4,
        out_specs=[anywhere] * 3,
        scratch_shapes=[
            V((toks, 4 * cap), BF), V((4 * cap, width), BF), V((toks, width), BF),
            V((2, toks), F32), V((3, cw, f), F32), pltpu.SemaphoreType.DMA((20,)),
        ],
    )(spots, both, gate_grad, weight_grad)
    return (input_grad, gate_grad.T, jnp.transpose(weight_grad, (1, 0, 2)))


def solution(mesh):
    in_specs = (
        P(("dp", "expert"), None),
        P(("dp", "expert"), None),
        P(("dp", "expert"), None),
        P(("dp", "expert"), None),
        P(None, "expert"),
        P(None, "expert"),
        P("expert", None),
    )
    out_specs = (P(("dp", "expert"), None), P(("dp", "expert"), None), P("dp", None, "expert"))
    return jax.shard_map(
        per_device, mesh=mesh, in_specs=in_specs, out_specs=out_specs, check_vma=False
    )
```

time: 85.6 us -> 72.7 us (0.85)
  the two profiles are of different devices: /device:TPU:24 before, /device:TPU:1 now
where the time goes in v2:
time: 72.7 us; the launch traced here: 72.5 us
  Pallas kernels  71.8 us (99%)
    pallas_call x1, Pallas kernels, per_device(): pl.pallas_call(functools.partial(kernel, nx, nz, cap), out_shape=[jax.Sha...  68.9 us
    pallas_call x1, Pallas kernels, per_device(): pl.pallas_call(finish, out_shape=[jax.ShapeDtypeStruct((toks, width), BF)...  2.98 us

profile of v2, /device:TPU:1, one launch (start us, length us, event | category | flops | bytes accessed | tf_op | source)
XLA Modules:
  0.0 72.5 jit_solution(5379916575680037446)
XLA Ops:
  0.6 68.9 %shard_map.94 = (bf16[48,3072]{1,0:T(8,128)(2,1)}, bf16[256,48]{1,0:T(8,128)(2,1)}, f32[2,256]{1,0:T(2,128)}, f32[3,32,256]{2,1,0:T(8,128)}) custom-call(s32[2,256]{1,0:T(2,128)} %bitcast.4, s32[2,256]{1,0:T(2,128)} %bitcast.5, bf16[256,3072]{1,0:T(8,128)(2,1)} %go_hbm.1, bf16[96,3072]{1,0:T(8,128)(2,1)} %x_hbm.1, bf16[3072,256]{1,0:T(8,128)(2,1)} %wg_hbm.1, ...), custom_call_target="tpu_custom_call" | custom-call | tf_op jit(solution)/shard_map/pallas_call | solution.py:458
  69.5 3.0 %shard_map.95 = (bf16[256,3072]{1,0:T(8,128)(2,1)}, f32[2,256]{1,0:T(2,128)}, f32[3,32,256]{2,1,0:T(8,128)}) custom-call(bf16[256,48]{1,0:T(8,128)(2,1)} %get-tuple-element.10.spots_hbm, bf16[48,3072]{1,0:T(8,128)(2,1)} %get-tuple-element.11.both_hbm, f32[2,256]{1,0:T(2,128)} %get-tuple-element.12.gg_hbm, f32[3,32,256]{2,1,0:T(8,128)} %get-tuple-element.13.wgr_hbm), custom_call_target="tpu_custom_call" | custom-call | tf_op jit(solution)/shard_map/pallas_call | solution.py:472

commit v3 on v2

--- a/solution.py
+++ b/solution.py
@@ -24,8 +24,8 @@
 def kernel(
     nx, nz, cap,
     routes_ref, levels_ref, go_hbm, x_hbm, wg_hbm, wu_hbm, wd_hbm,
-    both_ref, plt_ref, gg_ref, wgr_ref,
-    go, xv, wg, wu, wd,
+    both_hbm, plt_hbm, gg_hbm, wgr_hbm,
+    both, plt, gg, wgr, go, xv, wg, wu, wd,
     pl_ref, pk, pkx, zin, zinx, dyin, xp, xs, xty, act, hid, dfac,
     nar, gp_in, gm_in, g4_in, dab, hg, ip, ret, zsum, zrin, dyt,
     gds, gdr, gdo, psend, prr, msend, mrr, p0r, m0r, sd, gx, gxr, sx,
@@ -58,6 +58,13 @@
         return ((lax.rem(z + d, nz) * NY + y) * NC + core, ex)
 
     started = []
+    puts = []
+
+    def put(src, dst):
+        copy = pltpu.make_async_copy(src, dst, loc_sem.at[8 + len(puts)])
+        copy.start()
+        puts.append(copy)
+
 
     def send(src, dst, dev):
         i = len(started)
@@ -188,7 +195,8 @@
     dfac[...] = b_pre * sigma * (1.0 + a_pre * (1.0 - sigma))
     pl_two = jnp.concatenate(
         [pl_ref[...], pl_ref[...], jnp.zeros((LANES - 4 * cap, toks), F32)], axis=0)
-    plt_ref[...] = pl_two.T[:, :4 * cap].astype(BF)
+    plt[...] = pl_two.T[:, :4 * cap].astype(BF)
+    put(plt, plt_hbm)
 
     loads[3].wait()
     dy_other = []
@@ -222,17 +230,15 @@
         down.append([send(nar.at[i], gm_in.at[0, i], y_dev(NY - 1))])
 
     ip[:, :, width:] = jnp.broadcast_to(gate_part, (rows, LANES)).reshape(dyin.shape[0], SLAB, LANES)
-    halves = [(0, width // 2), (width // 2, width // 2 + LANES)]
-    back = [[], [], []]
-    for k, (a, w) in enumerate(halves):
-        for c in range(a, a + width // 2, 512):
-            part = nt(dab[:, :256], wg[c:c + 512, :]) + nt(dab[:, 256:], wu[c:c + 512, :])
-            ip[:, :, c:c + 512] = part.astype(BF).reshape(dyin.shape[0], SLAB, 512)
+    back = [[] for _ in range(5)]
+    for k, (a, w) in enumerate(cols):
+        part = nt(dab[:, :f], wg[a:a + quarter, :]) + nt(dab[:, f:], wu[a:a + quarter, :])
+        ip[:, :, a:a + quarter] = part.astype(BF).reshape(dyin.shape[0], SLAB, quarter)
         for d in range(1, nx):
             back[k].append(send(ip.at[lax.rem(x + d, nx) * NH + 1 - h, :, pl.ds(a, w)],
                                 ret.at[0, x, :, pl.ds(a, w)], x_dev(d)))
     for d in range(1, nx):
-        back[2].append(send(ip.at[lax.rem(x + d, nx) * NH + h], ret.at[1, x], x_dev(d)))
+        back[4].append(send(ip.at[lax.rem(x + d, nx) * NH + h], ret.at[1, x], x_dev(d)))
     ret[0, x] = ip[x * NH + 1 - h]
     ret[1, x] = ip[x * NH + h]
 
@@ -291,15 +297,17 @@
     z_back = []
 
     def cross(k):
-        a, w = halves[k]
+        a, w = cols[k]
         for copy in back[k]:
             copy.wait_recv()
         zsum[:, a:a + w] = nn(compact, ret[0, :, :, a:a + w].reshape(nx * SLAB, w)).astype(BF)
         z_back.append(send(zsum.at[:, pl.ds(a, w)], zrin.at[:, pl.ds(a, w)], h_dev))
 
     cross(0)
+    cross(1)
     pass_on(1)
-    cross(1)
+    cross(2)
+    cross(3)
     p_in[0].wait_recv()
     s3 = chip_sum(3)
     psend[1, 0:half] = (s3[0:half] + p0r[...].astype(F32)).astype(BF)
@@ -352,37 +360,42 @@
         zsd[d - 1] = sd[lax.rem(z + d, nz)].astype(BF)
         zd_in.append(send(zsd.at[d - 1], zrd.at[d - 1], z_dev(d)))
 
-    for copy in back[2]:
+    for copy in back[4]:
         copy.wait_recv()
-    for k, (a, w) in enumerate(halves):
+    for k, (a, w) in enumerate(cols):
         z_back[k].wait_recv()
         total = (nn(compact, ret[1, :, :, a:a + w].reshape(nx * SLAB, w))
                  + zrin[:, a:a + w].astype(F32))
-        n = width // 2
+        n = quarter
         high = total[:, :n].astype(BF)
-        both_ref[0:2 * cap, a:a + n] = high
-        both_ref[2 * cap:, a:a + n] = (total[:, :n] - high.astype(F32)).astype(BF)
+        both[0:2 * cap, a:a + n] = high
+        both[2 * cap:, a:a + n] = (total[:, :n] - high.astype(F32)).astype(BF)
+    put(both, both_hbm)
     gs2 = total[:, n:]
     prod = pl_ref[...] * jnp.concatenate([gs2, gs2], axis=1)
     top = lax.broadcasted_iota(jnp.int32, (2 * cap, toks), 0) < cap
     out = [jnp.sum(jnp.where(top, prod, 0.0), axis=0, keepdims=True),
            jnp.sum(jnp.where(top, 0.0, prod), axis=0, keepdims=True)]
-    gg_ref[0:1] = jnp.where(r0 == 0, out[0], 0.0) + jnp.where(r0 == 1, out[1], 0.0)
-    gg_ref[1:2] = jnp.where(r1 == 0, out[0], 0.0) + jnp.where(r1 == 1, out[1], 0.0)
+    gg[0:1] = jnp.where(r0 == 0, out[0], 0.0) + jnp.where(r0 == 1, out[1], 0.0)
+    gg[1:2] = jnp.where(r1 == 0, out[0], 0.0) + jnp.where(r1 == 1, out[1], 0.0)
+    put(gg, gg_hbm)
 
     acc = sx[z]
     for d in range(1, nz):
         zx_in[d - 1].wait_recv()
         acc = acc + zrx[d - 1].astype(F32)
-    wgr_ref[0] = acc[:, :256]
-    wgr_ref[1] = acc[:, 256:]
+    wgr[0] = acc[:, :256]
+    wgr[1] = acc[:, 256:]
     acc = sd[z]
     for d in range(1, nz):
         zd_in[d - 1].wait_recv()
         acc = acc + zrd[d - 1].astype(F32)
-    wgr_ref[2] = acc
+    wgr[2] = acc
+    put(wgr, wgr_hbm)
     for copy in started:
         copy.wait_send()
+    for copy in puts:
+        copy.wait()
 
 
 def finish(spots_hbm, both_hbm, gg_hbm, wgr_hbm, ig_hbm, gg_out, wgr_out,
@@ -433,6 +446,7 @@
     own = nz * cw
     V = pltpu.VMEM
     scratch = [
+        V((4 * cap, width), BF), V((toks, 4 * cap), BF), V((2, toks), F32), V((3, cw, f), F32),
         V((toks, width), BF), V((n_rows, width), BF), V((width, f), BF), V((width, f), BF),
         V((f, width), BF),
         V((2 * cap, toks), F32), V((2 * cap, ext), BF), V((2 * SLAB, ext), BF),
@@ -450,7 +464,7 @@
         V((nz, yw, 2 * f), F32), V((nz, cw, 2 * f), F32), V((nz, cw, 2 * f), F32),
         V((nz - 1, cw, f), BF), V((nz - 1, cw, f), BF),
         V((nz - 1, cw, 2 * f), BF), V((nz - 1, cw, 2 * f), BF),
-        pltpu.SemaphoreType.DMA((8,)), pltpu.SemaphoreType.DMA((100,)),
+        pltpu.SemaphoreType.DMA((16,)), pltpu.SemaphoreType.DMA((100,)),
         pltpu.SemaphoreType.DMA((100,)),
     ]
     vm = pl.BlockSpec(memory_space=pltpu.VMEM)
@@ -464,7 +478,7 @@
             jax.ShapeDtypeStruct((3, cw, f), F32),
         ],
         in_specs=[vm, vm] + [anywhere] * 5,
-        out_specs=[vm, vm, vm, vm],
+        out_specs=[anywhere] * 4,
         scratch_shapes=scratch,
         compiler_params=pltpu.CompilerParams(
             collective_id=0, has_side_effects=True, vmem_limit_bytes=56 * 1024 * 1024),

time: 72.7 us -> 72.5 us (level)
  no operation moved by 1% of the time
where the time goes in v3:
time: 72.5 us; the launch traced here: 72.3 us
  Pallas kernels  71.6 us (99%)
    pallas_call x1, Pallas kernels, per_device(): pl.pallas_call(functools.partial(kernel, nx, nz, cap), out_shape=[jax.Sha...  68.6 us
    pallas_call x1, Pallas kernels, per_device(): pl.pallas_call(finish, out_shape=[jax.ShapeDtypeStruct((toks, width), BF)...  3 us

profile of v3, /device:TPU:1, one launch (start us, length us, event | category | flops | bytes accessed | tf_op | source)
XLA Modules:
  0.0 72.3 jit_solution(13705324711210861156)
XLA Ops:
  0.6 68.6 %shard_map.94 = (bf16[48,3072]{1,0:T(8,128)(2,1)}, bf16[256,48]{1,0:T(8,128)(2,1)}, f32[2,256]{1,0:T(2,128)}, f32[3,32,256]{2,1,0:T(8,128)}) custom-call(s32[2,256]{1,0:T(2,128)} %bitcast.4, s32[2,256]{1,0:T(2,128)} %bitcast.5, bf16[256,3072]{1,0:T(8,128)(2,1)} %go_hbm.1, bf16[96,3072]{1,0:T(8,128)(2,1)} %x_hbm.1, bf16[3072,256]{1,0:T(8,128)(2,1)} %wg_hbm.1, ...), custom_call_target="tpu_custom_call" | custom-call | tf_op jit(solution)/shard_map/pallas_call | solution.py:472
  69.3 3.0 %shard_map.95 = (bf16[256,3072]{1,0:T(8,128)(2,1)}, f32[2,256]{1,0:T(2,128)}, f32[3,32,256]{2,1,0:T(8,128)}) custom-call(bf16[256,48]{1,0:T(8,128)(2,1)} %get-tuple-element.10.spots_hbm, bf16[48,3072]{1,0:T(8,128)(2,1)} %get-tuple-element.11.both_hbm, f32[2,256]{1,0:T(2,128)} %get-tuple-element.12.gg_hbm, f32[3,32,256]{2,1,0:T(8,128)} %get-tuple-element.13.wgr_hbm), custom_call_target="tpu_custom_call" | custom-call | tf_op jit(solution)/shard_map/pallas_call | solution.py:486
